TPU v7x, 512 devices: a whole 4x8x8 slice. The times are simulated.
512 devices in a mesh: group: 16 (over z, core), member: 32 (over y, x).
Axes of the slice: x: 4, y: 8, z: 8, core: 2. Of those that a mesh axis runs over, the one named last changes fastest.
Arguments:
- tokens: bfloat16 [8192, 7168], P('group', 'member'), may hold values from -6 to 6
- grad_output: bfloat16 [8192, 7168], P('group', 'member'), may hold values from -6 to 6
- gate_prob: bfloat16 [8192, 16], P('group'), may hold values from 0.099609375 to 1
- w_gate: bfloat16 [16, 7168, 1024], P('group', 'member'), may hold values from -0.0625 to 0.0625
- w_up: bfloat16 [16, 7168, 1024], P('group', 'member'), may hold values from -0.0625 to 0.0625
- w_down: bfloat16 [16, 1024, 7168], P('group', None, 'member'), may hold values from -0.1875 to 0.1875
- expert_slot: int32 [16], replicated, may hold values from 0 to 15, each once
- block_counts: int32 [16, 16], replicated, may hold values from 0 to 10, as said below
- block_lists: int32 [16, 16, 10], P('group'), may hold values from 0 to 15, as said below
Outputs:
- layer_output: bfloat16 [8192, 7168], P('group', 'member')
- grad_input: bfloat16 [8192, 7168], P('group', 'member')
- grad_w_gate: bfloat16 [16, 7168, 1024], P('group', 'member')
- grad_w_up: bfloat16 [16, 7168, 1024], P('group', 'member')
- grad_w_down: bfloat16 [16, 1024, 7168], P('group', None, 'member')
Inputs may be any that keep to these rules, and one draw needn't show every extreme that they name: `block_counts`: each group sends blocks to 1 to 2 experts and some group to exactly 2; each expert receives blocks from 1 to 2 groups and some expert from exactly 2; some count equals 10. `block_lists`: the first block_counts[g, e] entries of a list are distinct blocks of group g; later entries are block numbers that play no part. `expert_slot`: a permutation of the slots; slot s lies on group s.
All inputs are finite; a program needn't handle non-finite values.
Results may differ from a plain program's by a relative error of at most 0.034.
Values may be sent and summed in bfloat16 or wider, within the bound.
No kernel may reach another device: no remote copies, remote signals or barrier semaphores. Data moves between devices by JAX's collectives and lax.ppermute only.
A program may use at most 64 MiB of HBM per device.

v0:
```python
import jax
import jax.numpy as jnp
from jax import lax
from jax.sharding import PartitionSpec as P

MAXE = 2
BLK = 32


def expert_pass(input_rows, rows_dy, rows_p, gate_w, up_w, down_w):
    form_in, form_out, form_back, form_dx = (
        "xjb,bxl->xjl",
        "wzq,wqi->wzi",
        "eph,ezh->epz",
        "bya,qba->byq",
    )
    part_gate = jnp.einsum(form_in, input_rows, gate_w, preferred_element_type=jnp.float32)
    part_up = jnp.einsum(form_in, input_rows, up_w, preferred_element_type=jnp.float32)
    gate, up = (
        lax.psum(part_gate.astype(jnp.bfloat16), "member").astype(jnp.float32),
        lax.psum(part_up.astype(jnp.bfloat16), "member").astype(jnp.float32),
    )
    sigma = jax.nn.sigmoid(gate)
    hidden_state = (gate * sigma * up).astype(jnp.bfloat16)
    outcome = (
        rows_p[:, :, None]
        * jnp.einsum(form_out, hidden_state, down_w, preferred_element_type=jnp.float32)
    ).astype(jnp.bfloat16)
    gradient_rows = (rows_p[:, :, None] * rows_dy.astype(jnp.float32)).astype(jnp.bfloat16)
    part_hidden = jnp.einsum(form_back, gradient_rows, down_w, preferred_element_type=jnp.float32)
    grad_hidden = lax.psum(part_hidden.astype(jnp.bfloat16), "member").astype(jnp.float32)
    gate_gradient = (grad_hidden * up * sigma * (1.0 + gate * (1.0 - sigma))).astype(jnp.bfloat16)
    up_gradient = (grad_hidden * gate * sigma).astype(jnp.bfloat16)
    rows_dx = (
        jnp.einsum(form_dx, gate_gradient, gate_w, preferred_element_type=jnp.float32)
        + jnp.einsum(form_dx, up_gradient, up_w, preferred_element_type=jnp.float32)
    ).astype(jnp.bfloat16)
    weight_gate = jnp.einsum(
        "tgw,tgs->wts", input_rows, gate_gradient, preferred_element_type=jnp.float32
    ).astype(jnp.bfloat16)
    weight_up = jnp.einsum(
        "tgw,tgs->wts", input_rows, up_gradient, preferred_element_type=jnp.float32
    ).astype(jnp.bfloat16)
    weight_down = jnp.einsum(
        "sui,sug->sig", hidden_state, gradient_rows, preferred_element_type=jnp.float32
    ).astype(jnp.bfloat16)
    return (outcome, rows_dx, weight_gate, weight_up, weight_down)


def gather_rows(blocked, listed, keep_rows):
    picked = jnp.take(blocked, listed, axis=0)
    return picked * keep_rows[:, :, None, None].astype(blocked.dtype)


def place_rows(pieces, listed, keep_rows, block_total):
    placing = (
        (listed[:, :, None] == jnp.arange(block_total, dtype=jnp.int32)[None, None, :])
        & (keep_rows[:, :, None] > 0)
    ).astype(jnp.bfloat16)
    return jnp.einsum("kbn,kbtd->ntd", placing, pieces, preferred_element_type=jnp.float32)


def body(
    tokens, grad_output, gate_prob, w_gate, w_up, w_down, expert_slot, block_counts, block_lists
):
    width_share = tokens.shape[1]
    hidden_total = w_gate.shape[2]
    group_total = lax.axis_size("group")
    piece_size = hidden_total // group_total
    block_total = tokens.shape[0] // BLK
    entry_total = block_lists.shape[2]
    row_total = entry_total * BLK
    experts_total = block_counts.shape[1]
    group_index = lax.axis_index("group")
    entry_ids = jnp.arange(entry_total, dtype=jnp.int32)
    group_ids = jnp.arange(group_total, dtype=jnp.int32)
    ranks_wanted = jnp.arange(MAXE, dtype=jnp.int32)
    tok_blocks = tokens.reshape(block_total, BLK, width_share)
    grad_blocks = grad_output.reshape(block_total, BLK, width_share)
    prob_blocks = gate_prob.reshape(block_total, BLK, experts_total)
    my_counts = lax.dynamic_index_in_dim(block_counts, group_index, 0, keepdims=False)
    my_lists = block_lists[0]
    in_use = (block_counts > 0).astype(jnp.int32)
    use_rank = jnp.cumsum(in_use, axis=1) - 1
    selected = in_use[:, None, :] * (use_rank[:, None, :] == ranks_wanted[None, :, None]).astype(
        jnp.int32
    )
    need_slot = jnp.sum(selected * expert_slot[None, None, :], axis=2)
    need_valid = jnp.sum(selected, axis=2)
    own_select = lax.dynamic_index_in_dim(selected, group_index, 0, keepdims=False)
    my_amount = jnp.sum(own_select * my_counts[None, :], axis=1)
    listed = jnp.sum(own_select[:, :, None] * my_lists[None, :, :], axis=1)
    keep_rows = (entry_ids[None, :] < my_amount[:, None]).astype(jnp.int32)
    input_rows = gather_rows(tok_blocks, listed, keep_rows).reshape(MAXE, row_total, width_share)
    rows_dy = gather_rows(grad_blocks, listed, keep_rows).reshape(MAXE, row_total, width_share)
    prob_rows = gather_rows(prob_blocks, listed, keep_rows)
    rows_p = jnp.sum(
        prob_rows.astype(jnp.float32) * own_select[:, None, None, :].astype(jnp.float32), axis=3
    ).reshape(MAXE, row_total)
    gate_spread, up_spread, down_spread = (
        lax.all_to_all(
            w_gate[0].reshape(width_share, group_total, piece_size),
            "group",
            split_axis=1,
            concat_axis=1,
            tiled=True,
        ),
        lax.all_to_all(
            w_up[0].reshape(width_share, group_total, piece_size),
            "group",
            split_axis=1,
            concat_axis=1,
            tiled=True,
        ),
        lax.all_to_all(
            w_down.reshape(1, group_total, piece_size * width_share),
            "group",
            split_axis=1,
            concat_axis=1,
            tiled=True,
        ),
    )
    slot_order = need_slot.T
    gate_sent = jnp.take(gate_spread, slot_order, axis=1)
    up_sent = jnp.take(up_spread, slot_order, axis=1)
    down_sent = jnp.take(down_spread, slot_order, axis=1)
    gate_got, up_got, down_got = (
        lax.all_to_all(gate_sent, "group", split_axis=2, concat_axis=2, tiled=True),
        lax.all_to_all(up_sent, "group", split_axis=2, concat_axis=2, tiled=True),
        lax.all_to_all(down_sent, "group", split_axis=2, concat_axis=2, tiled=True),
    )
    outcome, rows_dx, weight_gate, weight_up, weight_down = expert_pass(
        input_rows,
        rows_dy,
        rows_p,
        gate_got.reshape(width_share, MAXE, hidden_total),
        up_got.reshape(width_share, MAXE, hidden_total),
        down_got.reshape(MAXE, hidden_total, width_share),
    )
    back_gate, back_up, back_down = (
        lax.all_to_all(
            weight_gate.reshape(width_share, MAXE, group_total, piece_size),
            "group",
            split_axis=2,
            concat_axis=2,
            tiled=True,
        ),
        lax.all_to_all(
            weight_up.reshape(width_share, MAXE, group_total, piece_size),
            "group",
            split_axis=2,
            concat_axis=2,
            tiled=True,
        ),
        lax.all_to_all(
            weight_down.reshape(1, MAXE, group_total, piece_size * width_share),
            "group",
            split_axis=2,
            concat_axis=2,
            tiled=True,
        ),
    )
    slot_match = (
        (slot_order[:, :, None] == group_ids[None, None, :]) & (need_valid.T[:, :, None] > 0)
    ).astype(jnp.bfloat16)
    summed_gate = jnp.einsum(
        "dmgk,mgs->dsk", back_gate, slot_match, preferred_element_type=jnp.float32
    ).astype(jnp.bfloat16)
    summed_up = jnp.einsum(
        "dmgk,mgs->dsk", back_up, slot_match, preferred_element_type=jnp.float32
    ).astype(jnp.bfloat16)
    summed_down = jnp.einsum(
        "amgq,mgs->asq", back_down, slot_match, preferred_element_type=jnp.float32
    ).astype(jnp.bfloat16)
    home_gate, home_up, home_down = (
        lax.all_to_all(summed_gate, "group", split_axis=1, concat_axis=1, tiled=True),
        lax.all_to_all(summed_up, "group", split_axis=1, concat_axis=1, tiled=True),
        lax.all_to_all(summed_down, "group", split_axis=1, concat_axis=1, tiled=True),
    )
    grad_w_gate = home_gate.reshape(1, width_share, hidden_total)
    grad_w_up = home_up.reshape(1, width_share, hidden_total)
    grad_w_down = home_down.reshape(1, hidden_total, width_share)
    out_blocks = place_rows(
        outcome.reshape(MAXE, entry_total, BLK, width_share), listed, keep_rows, block_total
    )
    dx_blocks = place_rows(
        rows_dx.reshape(MAXE, entry_total, BLK, width_share), listed, keep_rows, block_total
    )
    layer_output = out_blocks.reshape(block_total * BLK, width_share).astype(jnp.bfloat16)
    grad_input = dx_blocks.reshape(block_total * BLK, width_share).astype(jnp.bfloat16)
    return (layer_output, grad_input, grad_w_gate, grad_w_up, grad_w_down)


def solution(mesh):
    in_specs = (
        P("group", "member"),
        P("group", "member"),
        P("group", None),
        P("group", "member", None),
        P("group", "member", None),
        P("group", None, "member"),
        P(),
        P(),
        P("group", None, None),
    )
    out_specs = (
        P("group", "member"),
        P("group", "member"),
        P("group", "member", None),
        P("group", "member", None),
        P("group", None, "member"),
    )
    return jax.shard_map(body, mesh=mesh, in_specs=in_specs, out_specs=out_specs, check_vma=False)
```

profile of v0, /device:TPU:1, one launch (start us, length us, event | category | flops | bytes accessed | tf_op | source)
XLA Modules:
  0.0 531.6 jit_solution(10994055985351064944)
XLA Ops:
  7.2 1.2 copy.255
  8.4 1.2 reshape.285
  10.1 3.4 reduce.2
  13.6 1.1 reshape.287
  14.7 12.0 %all-to-all-start.4 = ((bf16[16,2,7168]{2,1,0:T(2,128)(2,1)}), bf16[16,2,7168]{2,1,0:T(2,128)(2,1)S(1)}, u32[]{:S(2)}, u32[]{:S(2)}) async-start(bf16[16,2,7168]{2,1,0:T(2,128)(2,1)} %reshape.287), calls=%async_computation.4 | async-start | bytes 917504 | tf_op jit(solution)/shard_map/all_to_all | solution.py:115
  26.6 1.0 copy.244
  27.8 14.8 %all-to-all-done.4 = bf16[16,2,7168]{2,1,0:T(2,128)(2,1)S(1)} async-done(((bf16[16,2,7168]{2,1,0:T(2,128)(2,1)}), bf16[16,2,7168]{2,1,0:T(2,128)(2,1)S(1)}, u32[]{:S(2)}, u32[]{:S(2)}) %all-to-all-start.4) | async-done | bytes 458784 | tf_op jit(solution)/shard_map/all_to_all | solution.py:115
  42.6 3.5 all-to-all-start
  46.9 1.0 copy.250
  48.6 1.1 gather_fusion.1
  49.7 13.0 %all-to-all-done = bf16[224,16,64]{0,2,1:T(8,128)(2,1)S(1)} async-done(((bf16[224,16,64]{0,2,1:T(8,128)(2,1)}), bf16[224,16,64]{0,2,1:T(8,128)(2,1)S(1)}, u32[]{:S(2)}, u32[]{:S(2)}) %all-to-all-start) | async-done | bytes 458784 | tf_op jit(solution)/shard_map/all_to_all | solution.py:101
  62.7 3.5 all-to-all-start.2
  66.2 2.5 broadcast_select_fusion
  68.7 14.2 %all-to-all-done.2 = bf16[224,16,64]{0,2,1:T(8,128)(2,1)S(1)} async-done(((bf16[224,16,64]{0,2,1:T(8,128)(2,1)}), bf16[224,16,64]{0,2,1:T(8,128)(2,1)S(1)}, u32[]{:S(2)}, u32[]{:S(2)}) %all-to-all-start.2) | async-done | bytes 458784 | tf_op jit(solution)/shard_map/all_to_all | solution.py:108
  82.9 4.2 all-to-all-start.5
  88.7 1.1 copy.252
  89.8 21.5 %all-to-all-done.5 = bf16[1,2,16,14336]{3,1,0,2:T(2,128)(2,1)} async-done(((bf16[1,2,16,14336]{3,1,0,2:T(2,128)(2,1)}), bf16[1,2,16,14336]{3,1,0,2:T(2,128)(2,1)}, u32[]{:S(2)}, u32[]{:S(2)}) %all-to-all-start.5) | async-done | bytes 917536 | tf_op jit(solution)/shard_map/all_to_all | solution.py:130
  111.3 3.6 all-to-all-start.3
  115.5 1.0 copy.246
  116.5 26.2 %all-to-all-done.3 = bf16[224,2,16,64]{0,3,1,2:T(8,128)(2,1)S(1)} async-done(((bf16[224,2,16,64]{0,3,1,2:T(8,128)(2,1)}), bf16[224,2,16,64]{0,3,1,2:T(8,128)(2,1)S(1)}, u32[]{:S(2)}, u32[]{:S(2)}) %all-to-all-start.3) | async-done | bytes 917536 | tf_op jit(solution)/shard_map/all_to_all | solution.py:129
  142.7 3.6 all-to-all-start.1
  149.9 2.4 copy.259
  152.3 3.4 reshape.188
  156.8 1.6 convolution_convert_fusion.1
  158.4 15.8 %all-to-all-done.1 = bf16[224,2,16,64]{0,3,1,2:T(8,128)(2,1)S(1)} async-done(((bf16[224,2,16,64]{0,3,1,2:T(8,128)(2,1)}), bf16[224,2,16,64]{0,3,1,2:T(8,128)(2,1)S(1)}, u32[]{:S(2)}, u32[]{:S(2)}) %all-to-all-start.1) | async-done | bytes 917536 | tf_op jit(solution)/shard_map/all_to_all | solution.py:128
  174.3 1.7 convolution_convert_fusion.2
  176.2 1.6 convolution_convert_fusion
  177.8 167.9 %all-reduce.3.cloned.1.call-done = (bf16[2,320,1024]{2,1,0:T(8,128)(2,1)}, bf16[2,320,1024]{2,1,0:T(8,128)(2,1)}, bf16[2,320,1024]{2,1,0:T(8,128)(2,1)}) async-done(((bf16[2,320,1024]{2,1,0:T(8,128)(2,1)}, bf16[2,320,1024]{2,1,0:T(8,128)(2,1)}, bf16[2,320,1024]{2,1,0:T(8,128)(2,1)}), (bf16[2,320,1024]{2,1,0:T(8,128)(2,1)}, bf16[2,320,1024]{2,1,0:T(8,128)(2,1)}, ...) | async-done | bytes 3932176 | tf_op jit(solution)/shard_map/psum | solution.py:21
  345.7 5.0 fusion.11
  350.7 1.6 fusion.12
  352.3 2.2 copy.273
  354.5 3.3 copy.274
  357.8 10.6 %all-to-all-start.6 = ((bf16[224,2,16,64]{0,1,3,2:T(2,128)(2,1)}), bf16[224,2,16,64]{0,1,3,2:T(2,128)(2,1)}, u32[]{:S(2)}, u32[]{:S(2)}) async-start(bf16[224,2,16,64]{0,1,3,2:T(2,128)(2,1)} %copy.274), calls=%async_computation.6 | async-start | bytes 2097152 | tf_op jit(solution)/shard_map/all_to_all | solution.py:141
  368.5 1.6 fusion.13
  370.1 2.3 copy.277
  372.3 3.3 copy.278
  375.6 20.9 %all-to-all-done.6 = bf16[224,2,16,64]{0,1,3,2:T(2,128)(2,1)} async-done(((bf16[224,2,16,64]{0,1,3,2:T(2,128)(2,1)}), bf16[224,2,16,64]{0,1,3,2:T(2,128)(2,1)}, u32[]{:S(2)}, u32[]{:S(2)}) %all-to-all-start.6) | async-done | bytes 917536 | tf_op jit(solution)/shard_map/all_to_all | solution.py:141
  396.5 4.4 all-to-all-start.8
  400.9 2.9 convolution_convert_fusion.3
  403.9 2.3 copy.281
  406.1 3.4 reshape.196
  409.5 3.1 copy.282
  412.6 15.6 %all-to-all-done.8 = bf16[224,2,16,64]{0,1,3,2:T(2,128)(2,1)} async-done(((bf16[224,2,16,64]{0,1,3,2:T(2,128)(2,1)}), bf16[224,2,16,64]{0,1,3,2:T(2,128)(2,1)}, u32[]{:S(2)}, u32[]{:S(2)}) %all-to-all-start.8) | async-done | bytes 917536 | tf_op jit(solution)/shard_map/all_to_all | solution.py:148
  428.2 4.2 all-to-all-start.10
  432.6 1.9 fusion.17
  435.5 21.7 %all-to-all-done.10 = bf16[1,2,16,14336]{3,1,0,2:T(2,128)(2,1)} async-done(((bf16[1,2,16,14336]{3,1,0,2:T(2,128)(2,1)}), bf16[1,2,16,14336]{3,1,0,2:T(2,128)(2,1)}, u32[]{:S(2)}, u32[]{:S(2)}) %all-to-all-start.10) | async-done | bytes 917536 | tf_op jit(solution)/shard_map/all_to_all | solution.py:155
  457.2 3.5 all-to-all-start.7
  460.6 1.9 fusion.16
  462.5 1.0 copy.280
  463.5 14.3 %all-to-all-done.7 = bf16[224,16,64]{0,2,1:T(8,128)(2,1)S(1)} async-done(((bf16[224,16,64]{0,2,1:T(8,128)(2,1)}), bf16[224,16,64]{0,2,1:T(8,128)(2,1)S(1)}, u32[]{:S(2)}, u32[]{:S(2)}) %all-to-all-start.7) | async-done | bytes 458784 | tf_op jit(solution)/shard_map/all_to_all | solution.py:176
  477.8 4.1 all-to-all-start.9
  482.0 2.6 fusion.52
  484.5 1.6 fusion.1
  486.8 4.2 reduce.3
  491.0 2.1 reshape.289
  493.2 5.0 all-to-all-done.9
  498.2 4.3 all-to-all-start.11
  502.5 1.7 fusion.19
  507.3 1.0 copy.287
  508.2 2.0 copy.288
  510.2 7.1 %all-to-all-done.11 = bf16[16,2,7168]{2,1,0:T(2,128)(2,1)} async-done(((bf16[16,2,7168]{2,1,0:T(2,128)(2,1)}), bf16[16,2,7168]{2,1,0:T(2,128)(2,1)}, u32[]{:S(2)}, u32[]{:S(2)}) %all-to-all-start.11) | async-done | bytes 458784 | tf_op jit(solution)/shard_map/all_to_all | solution.py:178
  517.3 2.9 reshape.290
  520.2 2.6 bitcast_reduce_fusion
  523.6 1.0 copy.289
  (92 shorter events, 14.9 us)
Async XLA Ops:
  10.1 16.5 %copy-start.8 = (bf16[1,224,1024]{2,1,0:T(8,128)(2,1)S(1)}, bf16[1,224,1024]{2,1,0:T(8,128)(2,1)}, u32[]{:S(2)}) copy-start(bf16[1,224,1024]{2,1,0:T(8,128)(2,1)} %param.16) | copy-start | bytes 1376260
  13.5 14.1 %copy-start.13 = (s32[16,16]{1,0:T(8,128)S(1)}, s32[16,16]{1,0:T(8,128)}, u32[]{:S(2)}) copy-start(s32[16,16]{1,0:T(8,128)} %param.20) | copy-start | bytes 3076
  14.7 31.4 %copy-start.15 = (s32[16]{0:T(128)S(1)}, s32[16]{0:T(128)}, u32[]{:S(2)}) copy-start(s32[16]{0:T(128)} %param.19) | copy-start | bytes 196
  14.7 32.2 %copy-start.9 = (bf16[1,224,1024]{2,1,0:T(8,128)(2,1)S(1)}, bf16[1,224,1024]{2,1,0:T(8,128)(2,1)}, u32[]{:S(2)}) copy-start(bf16[1,224,1024]{2,1,0:T(8,128)(2,1)} %param.17) | copy-start | bytes 1376260
  14.7 27.9 %all-to-all-start.4 = ((bf16[16,2,7168]{2,1,0:T(2,128)(2,1)}), bf16[16,2,7168]{2,1,0:T(2,128)(2,1)S(1)}, u32[]{:S(2)}, u32[]{:S(2)}) async-start(bf16[16,2,7168]{2,1,0:T(2,128)(2,1)} %reshape.287), calls=%async_computation.4 | async-start | bytes 917504 | tf_op jit(solution)/shard_map/all_to_all | solution.py:115
  42.6 20.1 %all-to-all-start = ((bf16[224,16,64]{0,2,1:T(8,128)(2,1)}), bf16[224,16,64]{0,2,1:T(8,128)(2,1)S(1)}, u32[]{:S(2)}, u32[]{:S(2)}) async-start(bf16[224,16,64]{0,2,1:T(8,128)(2,1)} %bitcast.9), calls=%async_computation | async-start | bytes 1048576 | tf_op jit(solution)/shard_map/all_to_all | solution.py:101
  62.7 20.2 %all-to-all-start.2 = ((bf16[224,16,64]{0,2,1:T(8,128)(2,1)}), bf16[224,16,64]{0,2,1:T(8,128)(2,1)S(1)}, u32[]{:S(2)}, u32[]{:S(2)}) async-start(bf16[224,16,64]{0,2,1:T(8,128)(2,1)} %bitcast.13), calls=%async_computation.2 | async-start | bytes 1048576 | tf_op jit(solution)/shard_map/all_to_all | solution.py:108
  82.9 28.4 %all-to-all-start.5 = ((bf16[1,2,16,14336]{3,1,0,2:T(2,128)(2,1)}), bf16[1,2,16,14336]{3,1,0,2:T(2,128)(2,1)}, u32[]{:S(2)}, u32[]{:S(2)}) async-start(bf16[1,2,16,14336]{3,1,0,2:T(2,128)(2,1)} %broadcast_select_fusion), calls=%async_computation.5 | async-start | bytes 1835008 | tf_op jit(solution)/shard_map/all_to_all | solution.py:130
  89.8 25.1 %copy-start.14 = (s32[1,16,10]{1,0,2:T(1,128)S(1)}, s32[1,16,10]{1,0,2:T(1,128)}, u32[]{:S(2)}) copy-start(s32[1,16,10]{1,0,2:T(1,128)} %param.21) | copy-start | bytes 1924
  111.3 31.4 %all-to-all-start.3 = ((bf16[224,2,16,64]{0,3,1,2:T(8,128)(2,1)}), bf16[224,2,16,64]{0,3,1,2:T(8,128)(2,1)S(1)}, u32[]{:S(2)}, u32[]{:S(2)}) async-start(bf16[224,2,16,64]{0,3,1,2:T(8,128)(2,1)} %copy.252), calls=%async_computation.3 | async-start | bytes 2097152 | tf_op jit(solution)/shard_map/all_to_all | solution.py:129
  116.5 30.5 %copy-start.12 = (bf16[512,16]{0,1:T(8,128)(2,1)S(1)}, bf16[512,16]{0,1:T(8,128)(2,1)}, u32[]{:S(2)}) copy-start(bf16[512,16]{0,1:T(8,128)(2,1)} %param.15) | copy-start | bytes 49156
  116.5 31.6 %copy-start.10 = (bf16[512,224]{0,1:T(8,128)(2,1)S(1)}, bf16[512,224]{0,1:T(8,128)(2,1)}, u32[]{:S(2)}) copy-start(bf16[512,224]{0,1:T(8,128)(2,1)} %param.13) | copy-start | bytes 688132
  116.5 31.8 %copy-start.11 = (bf16[512,224]{0,1:T(8,128)(2,1)S(1)}, bf16[512,224]{0,1:T(8,128)(2,1)}, u32[]{:S(2)}) copy-start(bf16[512,224]{0,1:T(8,128)(2,1)} %param.14) | copy-start | bytes 688132
  142.7 31.5 %all-to-all-start.1 = ((bf16[224,2,16,64]{0,3,1,2:T(8,128)(2,1)}), bf16[224,2,16,64]{0,3,1,2:T(8,128)(2,1)S(1)}, u32[]{:S(2)}, u32[]{:S(2)}) async-start(bf16[224,2,16,64]{0,3,1,2:T(8,128)(2,1)} %copy.246), calls=%async_computation.1 | async-start | bytes 2097152 | tf_op jit(solution)/shard_map/all_to_all | solution.py:128
  146.3 199.4 %all-reduce.3.cloned.1.call-start = ((), (), s32[]{:S(2)}) async-start(), calls=%async_computation.12 | async-start | bytes 7864320 | tf_op jit(solution)/shard_map/psum | solution.py:21
  155.8 1.0 copy-start
  174.3 1.7 copy-start.2
  174.3 1.9 copy-start.4
  357.8 38.7 %all-to-all-start.6 = ((bf16[224,2,16,64]{0,1,3,2:T(2,128)(2,1)}), bf16[224,2,16,64]{0,1,3,2:T(2,128)(2,1)}, u32[]{:S(2)}, u32[]{:S(2)}) async-start(bf16[224,2,16,64]{0,1,3,2:T(2,128)(2,1)} %copy.274), calls=%async_computation.6 | async-start | bytes 2097152 | tf_op jit(solution)/shard_map/all_to_all | solution.py:141
  396.5 31.7 %all-to-all-start.8 = ((bf16[224,2,16,64]{0,1,3,2:T(2,128)(2,1)}), bf16[224,2,16,64]{0,1,3,2:T(2,128)(2,1)}, u32[]{:S(2)}, u32[]{:S(2)}) async-start(bf16[224,2,16,64]{0,1,3,2:T(2,128)(2,1)} %copy.278), calls=%async_computation.8 | async-start | bytes 2097152 | tf_op jit(solution)/shard_map/all_to_all | solution.py:148
  428.2 28.9 %all-to-all-start.10 = ((bf16[1,2,16,14336]{3,1,0,2:T(2,128)(2,1)}), bf16[1,2,16,14336]{3,1,0,2:T(2,128)(2,1)}, u32[]{:S(2)}, u32[]{:S(2)}) async-start(bf16[1,2,16,14336]{3,1,0,2:T(2,128)(2,1)} %copy.282), calls=%async_computation.10 | async-start | bytes 1835008 | tf_op jit(solution)/shard_map/all_to_all | solution.py:155
  457.2 20.7 %all-to-all-start.7 = ((bf16[224,16,64]{0,2,1:T(8,128)(2,1)}), bf16[224,16,64]{0,2,1:T(8,128)(2,1)S(1)}, u32[]{:S(2)}, u32[]{:S(2)}) async-start(bf16[224,16,64]{0,2,1:T(8,128)(2,1)} %copy.276), calls=%async_computation.7 | async-start | bytes 1048576 | tf_op jit(solution)/shard_map/all_to_all | solution.py:176
  477.8 6.7 %copy-start.6 = (bf16[224,16,64]{0,2,1:T(8,128)(2,1)}, bf16[224,16,64]{0,2,1:T(8,128)(2,1)S(1)}, u32[]{:S(2)}) copy-start(bf16[224,16,64]{0,2,1:T(8,128)(2,1)S(1)} %all-to-all-done.7) | copy-start | bytes 1376260
  477.8 20.3 %all-to-all-start.9 = ((bf16[224,16,64]{0,2,1:T(8,128)(2,1)}), bf16[224,16,64]{0,2,1:T(8,128)(2,1)}, u32[]{:S(2)}, u32[]{:S(2)}) async-start(bf16[224,16,64]{0,2,1:T(8,128)(2,1)} %copy.280), calls=%async_computation.9 | async-start | bytes 1048576 | tf_op jit(solution)/shard_map/all_to_all | solution.py:177
  486.8 15.7 %copy-start.1 = (bf16[224,2,16,64]{0,3,2,1:T(8,128)(2,1)S(1)}, bf16[224,2,16,64]{0,3,2,1:T(8,128)(2,1)}, u32[]{:S(2)}) copy-start(bf16[224,2,16,64]{0,3,2,1:T(8,128)(2,1)} %copy-done) | copy-start | bytes 2752516
  498.2 19.2 %all-to-all-start.11 = ((bf16[16,2,7168]{2,1,0:T(2,128)(2,1)}), bf16[16,2,7168]{2,1,0:T(2,128)(2,1)}, u32[]{:S(2)}, u32[]{:S(2)}) async-start(bf16[16,2,7168]{2,1,0:T(2,128)(2,1)} %reshape.289), calls=%async_computation.11 | async-start | bytes 917504 | tf_op jit(solution)/shard_map/all_to_all | solution.py:178
  502.5 2.9 copy-start.5
  504.2 1.3 copy-start.3
  506.0 1.2 copy-start.7
Sparse Core Ops, SparseCore 0:
  177.9 167.7 all-reduce.2
where the time goes:
time: 540 us; the launch traced here: 532 us
  waiting for transfers between devices  358 us (66%)
  starting transfers between devices  61.9 us (11%)
  local copies, waits for them, and re-layouts  58.1 us (11%)
  matrix products  21.8 us (4%)
  other arithmetic  17.1 us (3%)
  between operations  14.8 us (3%)
    psum x1, waiting for transfers between devices, expert_pass(): lax.psum(part_up.astype(jnp.bfloat16), 'member').astype(jnp.float32)  168 us
    all_to_all x1, waiting for transfers between devices, body(): lax.all_to_all(up_sent, 'group', split_axis=2, concat_axis=2, tiled=True)  26.2 us
    all_to_all x1, waiting for transfers between devices, body(): lax.all_to_all(weight_down.reshape(1, MAXE, group_total, piece_size * wid...  21.7 us
    all_to_all x1, waiting for transfers between devices, body(): lax.all_to_all(down_sent, 'group', split_axis=2, concat_axis=2, tiled=True)  21.5 us
    all_to_all x1, waiting for transfers between devices, body(): lax.all_to_all(weight_gate.reshape(width_share, MAXE, group_total, piece_...  20.9 us
    unnamed x49, local copies, waits for them, and re-layouts  17.7 us
    all_to_all x1, waiting for transfers between devices, body(): lax.all_to_all(gate_sent, 'group', split_axis=2, concat_axis=2, tiled=True)  15.8 us
    all_to_all x1, waiting for transfers between devices, body(): lax.all_to_all(weight_up.reshape(width_share, MAXE, group_total, piece_si...  15.6 us
  transfers between devices with their start and end apart: 13, of which 13 were waited for; matrix products, arithmetic and copies ran while one was open for 12% of the time, Pallas kernels for 0%

commit v1 on v0

--- a/solution.py
+++ b/solution.py
@@ -8,6 +8,10 @@
 
 
 def expert_pass(input_rows, rows_dy, rows_p, gate_w, up_w, down_w):
+
+    def name_streams(field):
+        return lax.all_gather(field, "member").sum(axis=0)
+
     form_in, form_out, form_back, form_dx = (
         "xjb,bxl->xjl",
         "wzq,wqi->wzi",
@@ -18,7 +22,7 @@
     part_up = jnp.einsum(form_in, input_rows, up_w, preferred_element_type=jnp.float32)
     gate, up = (
         lax.psum(part_gate.astype(jnp.bfloat16), "member").astype(jnp.float32),
-        lax.psum(part_up.astype(jnp.bfloat16), "member").astype(jnp.float32),
+        name_streams(part_up.astype(jnp.bfloat16)).astype(jnp.float32),
     )
     sigma = jax.nn.sigmoid(gate)
     hidden_state = (gate * sigma * up).astype(jnp.bfloat16)

time: 540 us -> 741 us (1.37)
  waiting for transfers between devices: 358 us -> 527 us
  blocking collectives: 0 us -> 19.3 us
  other arithmetic: 17.1 us -> 34.8 us
    all_gather x0 -> x1, waiting for transfers between devices: none -> 192 us  [name_streams(): return lax.all_gather(field, 'member').sum(axis=0)]
    all_to_all x0 -> x1, blocking collectives: none -> 19.3 us  [body(): lax.all_to_all(w_down.reshape(1, group_total, piece_size * width_share),...]
    psum x1, waiting for transfers between devices: 168 us -> 150 us  [expert_pass(): lax.psum(part_gate.astype(jnp.bfloat16), 'member').astype(jnp.float32)]
    reduce_sum x0 -> x1, other arithmetic: none -> 15 us  [name_streams(): return lax.all_gather(field, 'member').sum(axis=0)]
    all_to_all x1 -> x0, waiting for transfers between devices: 14.8 us -> none  [body(): lax.all_to_all(w_down.reshape(1, group_total, piece_size * width_share),...]
    all_to_all x1 -> x0, starting transfers between devices: 12 us -> none  [body(): lax.all_to_all(w_down.reshape(1, group_total, piece_size * width_share),...]
    all_to_all x1, starting transfers between devices: 3.47 us -> 12 us  [body(): lax.all_to_all(w_gate[0].reshape(width_share, group_total, piece_size), '...]
    all_to_all x1, waiting for transfers between devices: 15.8 us -> 23.5 us  [body(): lax.all_to_all(gate_sent, 'group', split_axis=2, concat_axis=2, tiled=True)]
  transfers between devices with their start and end apart: 13 -> 13, of which waited for: 13 -> 13; matrix products, arithmetic and copies ran while one was open for 12% -> 11% of each run, Pallas kernels for 0% -> 0%
where the time goes in v1:
time: 741 us; the launch traced here: 732 us
  waiting for transfers between devices  527 us (71%)
  starting transfers between devices  59.2 us (8%)
  local copies, waits for them, and re-layouts  55 us (7%)
  other arithmetic  34.8 us (5%)
  matrix products  21.8 us (3%)
  blocking collectives  19.3 us (3%)
  between operations  14.8 us (2%)
    all_gather x1, waiting for transfers between devices, name_streams(): return lax.all_gather(field, 'member').sum(axis=0)  192 us
    psum x1, waiting for transfers between devices, expert_pass(): lax.psum(part_gate.astype(jnp.bfloat16), 'member').astype(jnp.float32)  150 us
    all_to_all x1, waiting for transfers between devices, body(): lax.all_to_all(up_sent, 'group', split_axis=2, concat_axis=2, tiled=True)  24.7 us
    all_to_all x1, waiting for transfers between devices, body(): lax.all_to_all(down_sent, 'group', split_axis=2, concat_axis=2, tiled=True)  23.5 us
    all_to_all x1, waiting for transfers between devices, body(): lax.all_to_all(gate_sent, 'group', split_axis=2, concat_axis=2, tiled=True)  23.5 us
    all_to_all x1, waiting for transfers between devices, body(): lax.all_to_all(weight_down.reshape(1, MAXE, group_total, piece_size * wid...  21.6 us
    all_to_all x1, waiting for transfers between devices, body(): lax.all_to_all(weight_gate.reshape(width_share, MAXE, group_total, piece_...  20.9 us
    all_to_all x1, blocking collectives, body(): lax.all_to_all(w_down.reshape(1, group_total, piece_size * width_share),...  19.3 us
  transfers between devices with their start and end apart: 13, of which 13 were waited for; matrix products, arithmetic and copies ran while one was open for 11% of the time, Pallas kernels for 0%

profile of v1, /device:TPU:1, one launch (start us, length us, event | category | flops | bytes accessed | tf_op | source)
XLA Modules:
  0.0 731.9 jit_solution(9866844518494905146)
XLA Ops:
  7.2 2.1 copy.244
  9.3 12.0 %all-to-all-start = ((bf16[224,16,64]{0,2,1:T(8,128)(2,1)}), bf16[224,16,64]{0,2,1:T(8,128)(2,1)S(1)}, u32[]{:S(2)}, u32[]{:S(2)}) async-start(bf16[224,16,64]{0,2,1:T(8,128)(2,1)} %bitcast.9), calls=%async_computation | async-start | bytes 1048576 | tf_op jit(solution)/shard_map/all_to_all | solution.py:105
  21.2 1.0 copy.250
  22.4 16.1 %all-to-all-done = bf16[224,16,64]{0,2,1:T(8,128)(2,1)S(1)} async-done(((bf16[224,16,64]{0,2,1:T(8,128)(2,1)}), bf16[224,16,64]{0,2,1:T(8,128)(2,1)S(1)}, u32[]{:S(2)}, u32[]{:S(2)}) %all-to-all-start) | async-done | bytes 458784 | tf_op jit(solution)/shard_map/all_to_all | solution.py:105
  38.6 3.5 all-to-all-start.2
  43.6 15.1 %all-to-all-done.2 = bf16[224,16,64]{0,2,1:T(8,128)(2,1)S(1)} async-done(((bf16[224,16,64]{0,2,1:T(8,128)(2,1)}), bf16[224,16,64]{0,2,1:T(8,128)(2,1)S(1)}, u32[]{:S(2)}, u32[]{:S(2)}) %all-to-all-start.2) | async-done | bytes 458784 | tf_op jit(solution)/shard_map/all_to_all | solution.py:112
  59.4 1.2 select_bitcast_fusion.1
  60.6 1.1 copy.252
  61.7 3.7 all-to-all-start.3
  67.9 24.7 %all-to-all-done.3 = bf16[224,2,16,64]{0,3,1,2:T(8,128)(2,1)S(1)} async-done(((bf16[224,2,16,64]{0,3,1,2:T(8,128)(2,1)}), bf16[224,2,16,64]{0,3,1,2:T(8,128)(2,1)S(1)}, u32[]{:S(2)}, u32[]{:S(2)}) %all-to-all-start.3) | async-done | bytes 917536 | tf_op jit(solution)/shard_map/all_to_all | solution.py:133
  93.7 1.6 convolution_convert_fusion.1
  95.4 1.0 copy-done.11
  96.6 1.2 reshape.286
  98.3 3.4 reduce.3
  102.0 19.3 %all_to_all.60 = bf16[16,2,7168]{2,1,0:T(2,128)(2,1)S(1)} all-to-all(bf16[16,2,7168]{2,1,0:T(2,128)(2,1)S(1)} %reshape.288), channel_id=1, replica_groups=mesh['group'=16,'member'=32] {'group'}, dimensions={0} | all-to-all | bytes 917504 | tf_op jit(solution)/shard_map/all_to_all | solution.py:119
  122.0 1.1 gather_fusion.1
  123.1 2.5 broadcast_select_fusion
  125.6 3.7 all-to-all-start.5
  129.3 1.1 copy.246
  130.3 23.5 %all-to-all-done.5 = bf16[1,2,16,14336]{3,1,0,2:T(2,128)(2,1)S(1)} async-done(((bf16[1,2,16,14336]{3,1,0,2:T(2,128)(2,1)}), bf16[1,2,16,14336]{3,1,0,2:T(2,128)(2,1)S(1)}, u32[]{:S(2)}, u32[]{:S(2)}) %all-to-all-start.5) | async-done | bytes 917536 | tf_op jit(solution)/shard_map/all_to_all | solution.py:134
  153.9 3.6 all-to-all-start.1
  160.1 1.5 reshape.188
  161.6 23.5 %all-to-all-done.1 = bf16[224,2,16,64]{0,3,1,2:T(8,128)(2,1)S(1)} async-done(((bf16[224,2,16,64]{0,3,1,2:T(8,128)(2,1)}), bf16[224,2,16,64]{0,3,1,2:T(8,128)(2,1)S(1)}, u32[]{:S(2)}, u32[]{:S(2)}) %all-to-all-start.1) | async-done | bytes 917536 | tf_op jit(solution)/shard_map/all_to_all | solution.py:132
  185.3 1.6 convolution_convert_fusion.2
  186.9 1.6 convolution_convert_fusion
  188.6 191.6 %all-gather.3.cloned.1.call-done = bf16[64,320,1024]{2,1,0:T(8,128)(2,1)} async-done(((bf16[2,320,1024]{2,1,0:T(8,128)(2,1)}), bf16[64,320,1024]{2,1,0:T(8,128)(2,1)}) %all-gather.3.cloned.1.call-update) | async-done | bytes 41943056 | tf_op jit(solution)/shard_map/all_gather | solution.py:13
  380.2 15.0 %reduce_sum.64 = bf16[2,320,1024]{2,1,0:T(8,128)(2,1)} reduce(bf16[32,2,320,1024]{3,2,1,0:T(8,128)(2,1)} %bitcast.131, bf16[]{:T(256)} %constant.78.clone.1), dimensions={0}, to_apply=%region_6.9 | reduce | flops 20316160 | bytes 43253760 | tf_op jit(solution)/shard_map/reduce_sum | solution.py:13
  395.2 149.7 %all-reduce.3.cloned.1.call-done = (bf16[2,320,1024]{2,1,0:T(8,128)(2,1)}, bf16[2,320,1024]{2,1,0:T(8,128)(2,1)}) async-done(((bf16[2,320,1024]{2,1,0:T(8,128)(2,1)}, bf16[2,320,1024]{2,1,0:T(8,128)(2,1)}), (bf16[2,320,1024]{2,1,0:T(8,128)(2,1)}, bf16[2,320,1024]{2,1,0:T(8,128)(2,1)})) %all-reduce.3.cloned.1.call-update) | async-done | bytes 2621456 | tf_op jit(solution)/shard_map/psum | solution.py:24
  544.9 5.0 fusion.11
  549.8 1.6 fusion.12
  551.5 2.2 copy.273
  553.7 3.3 copy.274
  556.9 11.7 %all-to-all-start.6 = ((bf16[224,2,16,64]{0,1,3,2:T(2,128)(2,1)}), bf16[224,2,16,64]{0,1,3,2:T(2,128)(2,1)}, u32[]{:S(2)}, u32[]{:S(2)}) async-start(bf16[224,2,16,64]{0,1,3,2:T(2,128)(2,1)} %copy.274), calls=%async_computation.6 | async-start | bytes 2097152 | tf_op jit(solution)/shard_map/all_to_all | solution.py:145
  568.7 1.6 fusion.13
  570.3 2.3 copy.277
  572.6 3.3 copy.278
  575.9 20.9 %all-to-all-done.6 = bf16[224,2,16,64]{0,1,3,2:T(2,128)(2,1)} async-done(((bf16[224,2,16,64]{0,1,3,2:T(2,128)(2,1)}), bf16[224,2,16,64]{0,1,3,2:T(2,128)(2,1)}, u32[]{:S(2)}, u32[]{:S(2)}) %all-to-all-start.6) | async-done | bytes 917536 | tf_op jit(solution)/shard_map/all_to_all | solution.py:145
  596.7 4.4 all-to-all-start.8
  601.1 2.9 convolution_convert_fusion.3
  604.1 2.3 copy.281
  606.3 3.4 reshape.196
  609.7 3.1 copy.282
  612.8 15.7 %all-to-all-done.8 = bf16[224,2,16,64]{0,1,3,2:T(2,128)(2,1)} async-done(((bf16[224,2,16,64]{0,1,3,2:T(2,128)(2,1)}), bf16[224,2,16,64]{0,1,3,2:T(2,128)(2,1)}, u32[]{:S(2)}, u32[]{:S(2)}) %all-to-all-start.8) | async-done | bytes 917536 | tf_op jit(solution)/shard_map/all_to_all | solution.py:152
  628.4 4.2 all-to-all-start.10
  632.8 1.9 fusion.17
  634.7 1.0 copy.276
  635.7 21.6 %all-to-all-done.10 = bf16[1,2,16,14336]{3,1,0,2:T(2,128)(2,1)} async-done(((bf16[1,2,16,14336]{3,1,0,2:T(2,128)(2,1)}), bf16[1,2,16,14336]{3,1,0,2:T(2,128)(2,1)}, u32[]{:S(2)}, u32[]{:S(2)}) %all-to-all-start.10) | async-done | bytes 917536 | tf_op jit(solution)/shard_map/all_to_all | solution.py:159
  657.4 3.5 all-to-all-start.7
  660.8 1.9 fusion.16
  662.7 1.0 copy.280
  663.7 14.3 %all-to-all-done.7 = bf16[224,16,64]{0,2,1:T(8,128)(2,1)S(1)} async-done(((bf16[224,16,64]{0,2,1:T(8,128)(2,1)}), bf16[224,16,64]{0,2,1:T(8,128)(2,1)S(1)}, u32[]{:S(2)}, u32[]{:S(2)}) %all-to-all-start.7) | async-done | bytes 458784 | tf_op jit(solution)/shard_map/all_to_all | solution.py:180
  678.0 4.1 all-to-all-start.9
  682.2 2.6 fusion.52
  684.7 1.6 fusion.1
  686.3 1.7 copy.320
  688.0 5.3 reduce.4
  693.2 2.1 reshape.290
  695.4 3.0 all-to-all-done.9
  698.4 4.3 all-to-all-start.11
  704.6 1.7 fusion.18
  708.5 2.0 copy.288
  710.5 7.1 all-to-all-done.11
  717.6 2.9 reshape.291
  720.5 2.6 bitcast_reduce_fusion
  (99 shorter events, 16.2 us)
Async XLA Ops:
  7.2 14.1 %copy-start.10 = (bf16[1,224,1024]{2,1,0:T(8,128)(2,1)S(1)}, bf16[1,224,1024]{2,1,0:T(8,128)(2,1)}, u32[]{:S(2)}) copy-start(bf16[1,224,1024]{2,1,0:T(8,128)(2,1)} %param.17) | copy-start | bytes 1376260
  7.2 15.1 %copy-start.15 = (s32[16,16]{1,0:T(8,128)S(1)}, s32[16,16]{1,0:T(8,128)}, u32[]{:S(2)}) copy-start(s32[16,16]{1,0:T(8,128)} %param.20) | copy-start | bytes 3076
  9.3 32.8 %copy-start.17 = (s32[16]{0:T(128)S(1)}, s32[16]{0:T(128)}, u32[]{:S(2)}) copy-start(s32[16]{0:T(128)} %param.19) | copy-start | bytes 196
  9.3 29.3 %all-to-all-start = ((bf16[224,16,64]{0,2,1:T(8,128)(2,1)}), bf16[224,16,64]{0,2,1:T(8,128)(2,1)S(1)}, u32[]{:S(2)}, u32[]{:S(2)}) async-start(bf16[224,16,64]{0,2,1:T(8,128)(2,1)} %bitcast.9), calls=%async_computation | async-start | bytes 1048576 | tf_op jit(solution)/shard_map/all_to_all | solution.py:105
  38.6 20.2 %all-to-all-start.2 = ((bf16[224,16,64]{0,2,1:T(8,128)(2,1)}), bf16[224,16,64]{0,2,1:T(8,128)(2,1)S(1)}, u32[]{:S(2)}, u32[]{:S(2)}) async-start(bf16[224,16,64]{0,2,1:T(8,128)(2,1)} %bitcast.13), calls=%async_computation.2 | async-start | bytes 1048576 | tf_op jit(solution)/shard_map/all_to_all | solution.py:112
  61.7 3.8 copy-start.16
  61.7 4.4 copy-start.12
  61.7 4.6 copy-start.13
  61.7 31.0 %all-to-all-start.3 = ((bf16[224,2,16,64]{0,3,1,2:T(8,128)(2,1)}), bf16[224,2,16,64]{0,3,1,2:T(8,128)(2,1)S(1)}, u32[]{:S(2)}, u32[]{:S(2)}) async-start(bf16[224,2,16,64]{0,3,1,2:T(8,128)(2,1)} %copy.252), calls=%async_computation.3 | async-start | bytes 2097152 | tf_op jit(solution)/shard_map/all_to_all | solution.py:133
  65.4 314.8 %all-gather.3.cloned.1.call-start = ((), (), s32[]{:S(2)}) async-start(), calls=%async_computation.12 | async-start | bytes 43253760 | tf_op jit(solution)/shard_map/all_gather | solution.py:13
  92.8 1.0 copy-start
  95.4 1.0 copy-start.11
  125.6 3.7 copy-start.4
  125.6 28.3 %all-to-all-start.5 = ((bf16[1,2,16,14336]{3,1,0,2:T(2,128)(2,1)}), bf16[1,2,16,14336]{3,1,0,2:T(2,128)(2,1)S(1)}, u32[]{:S(2)}, u32[]{:S(2)}) async-start(bf16[1,2,16,14336]{3,1,0,2:T(2,128)(2,1)} %broadcast_select_fusion), calls=%async_computation.5 | async-start | bytes 1835008 | tf_op jit(solution)/shard_map/all_to_all | solution.py:134
  130.3 27.7 %copy-start.14 = (bf16[512,16]{0,1:T(8,128)(2,1)S(1)}, bf16[512,16]{0,1:T(8,128)(2,1)}, u32[]{:S(2)}) copy-start(bf16[512,16]{0,1:T(8,128)(2,1)} %param.15) | copy-start | bytes 49156
  153.9 31.3 %all-to-all-start.1 = ((bf16[224,2,16,64]{0,3,1,2:T(8,128)(2,1)}), bf16[224,2,16,64]{0,3,1,2:T(8,128)(2,1)S(1)}, u32[]{:S(2)}, u32[]{:S(2)}) async-start(bf16[224,2,16,64]{0,3,1,2:T(8,128)(2,1)} %copy.246), calls=%async_computation.1 | async-start | bytes 2097152 | tf_op jit(solution)/shard_map/all_to_all | solution.py:132
  157.4 387.5 %all-reduce.3.cloned.1.call-start = ((), (), s32[]{:S(2)}) async-start(), calls=%async_computation.13 | async-start | bytes 5242880 | tf_op jit(solution)/shard_map/psum | solution.py:24
  161.6 25.3 %copy-start.5 = (bf16[2,1024,224]{2,1,0:T(8,128)(2,1)}, bf16[2,1024,224]{2,1,0:T(8,128)(2,1)S(1)}, u32[]{:S(2)}) copy-start(bf16[2,1024,224]{2,1,0:T(8,128)(2,1)S(1)} %reshape.188) | copy-start | bytes 2752516
  185.3 1.7 copy-start.2
  185.3 1.7 copy-start.6
  556.9 39.8 %all-to-all-start.6 = ((bf16[224,2,16,64]{0,1,3,2:T(2,128)(2,1)}), bf16[224,2,16,64]{0,1,3,2:T(2,128)(2,1)}, u32[]{:S(2)}, u32[]{:S(2)}) async-start(bf16[224,2,16,64]{0,1,3,2:T(2,128)(2,1)} %copy.274), calls=%async_computation.6 | async-start | bytes 2097152 | tf_op jit(solution)/shard_map/all_to_all | solution.py:145
  596.7 31.7 %all-to-all-start.8 = ((bf16[224,2,16,64]{0,1,3,2:T(2,128)(2,1)}), bf16[224,2,16,64]{0,1,3,2:T(2,128)(2,1)}, u32[]{:S(2)}, u32[]{:S(2)}) async-start(bf16[224,2,16,64]{0,1,3,2:T(2,128)(2,1)} %copy.278), calls=%async_computation.8 | async-start | bytes 2097152 | tf_op jit(solution)/shard_map/all_to_all | solution.py:152
  628.4 28.9 %all-to-all-start.10 = ((bf16[1,2,16,14336]{3,1,0,2:T(2,128)(2,1)}), bf16[1,2,16,14336]{3,1,0,2:T(2,128)(2,1)}, u32[]{:S(2)}, u32[]{:S(2)}) async-start(bf16[1,2,16,14336]{3,1,0,2:T(2,128)(2,1)} %copy.282), calls=%async_computation.10 | async-start | bytes 1835008 | tf_op jit(solution)/shard_map/all_to_all | solution.py:159
  657.4 20.7 %all-to-all-start.7 = ((bf16[224,16,64]{0,2,1:T(8,128)(2,1)}), bf16[224,16,64]{0,2,1:T(8,128)(2,1)S(1)}, u32[]{:S(2)}, u32[]{:S(2)}) async-start(bf16[224,16,64]{0,2,1:T(8,128)(2,1)} %copy.276), calls=%async_computation.7 | async-start | bytes 1048576 | tf_op jit(solution)/shard_map/all_to_all | solution.py:180
  678.0 6.7 copy-start.8
  678.0 20.3 %all-to-all-start.9 = ((bf16[224,16,64]{0,2,1:T(8,128)(2,1)}), bf16[224,16,64]{0,2,1:T(8,128)(2,1)}, u32[]{:S(2)}, u32[]{:S(2)}) async-start(bf16[224,16,64]{0,2,1:T(8,128)(2,1)} %copy.280), calls=%async_computation.9 | async-start | bytes 1048576 | tf_op jit(solution)/shard_map/all_to_all | solution.py:181
  688.0 14.7 %copy-start.1 = (bf16[224,2,16,64]{0,3,2,1:T(8,128)(2,1)S(1)}, bf16[224,2,16,64]{0,3,2,1:T(8,128)(2,1)}, u32[]{:S(2)}) copy-start(bf16[224,2,16,64]{0,3,2,1:T(8,128)(2,1)} %copy-done) | copy-start | bytes 2752516
  688.0 14.7 %copy-start.7 = (f32[2,320,224]{2,1,0:T(8,128)S(1)}, f32[2,320,224]{2,1,0:T(8,128)}, u32[]{:S(2)}) copy-start(f32[2,320,224]{2,1,0:T(8,128)} %fusion.52) | copy-start | bytes 1720324
  698.4 19.3 %all-to-all-start.11 = ((bf16[16,2,7168]{2,1,0:T(2,128)(2,1)}), bf16[16,2,7168]{2,1,0:T(2,128)(2,1)}, u32[]{:S(2)}, u32[]{:S(2)}) async-start(bf16[16,2,7168]{2,1,0:T(2,128)(2,1)} %reshape.290), calls=%async_computation.11 | async-start | bytes 917504 | tf_op jit(solution)/shard_map/all_to_all | solution.py:182
  703.2 1.3 copy-start.3
  706.3 1.2 copy-start.9
Sparse Core Ops, SparseCore 0:
  95.5 284.6 all-gather.2
  383.9 160.9 all-reduce.2
